TPU v7x, 32 devices: a whole 2x2x4 slice. The times are simulated.
32 devices in a mesh: ens: 2 (over x), lat: 4 (over z), lon: 4 (over y, core).
Axes of the slice: x: 2, y: 2, z: 4, core: 2. Of those that a mesh axis runs over, the one named last changes fastest.
Arguments:
- prior_states: bfloat16 [16, 40, 128, 1024], P('ens', None, 'lat', 'lon'), may hold values from -6 to 6
- measured_brightness: float32 [16, 64, 512], P(None, 'lat', 'lon'), may hold values from -16 to 16
- measured_indicator: int32 [64, 512], P('lat', 'lon'), may hold values 0 or 1
- sensor_error_spread: float32 [16], replicated, may hold values from 2 to 8
- entry_layer_stencil: bfloat16 [64, 40, 5, 5], replicated, may hold values from -0.25 to 0.25
- entry_layer_offset: float32 [64], replicated, may hold values from -3 to 3
- middle_layer_stencil: bfloat16 [64, 64, 3, 3], replicated, may hold values from -0.375 to 0.375
- middle_layer_offset: float32 [64], replicated, may hold values from -3 to 3
- brightness_matrix: bfloat16 [16, 64], replicated, may hold values from -0.75 to 0.75
- brightness_offset: float32 [16], replicated, may hold values from -3 to 3
- ancestor_indices: int32 [16, 4, 8], P(None, 'lat', 'lon'), may hold values from 0 to 15, as said below
Outputs:
- analysis: float32 [16, 40, 128, 1024], P('ens', None, 'lat', 'lon')
- weights: float32 [16, 64, 512], P('ens', 'lat', 'lon')
Inputs may be any that keep to these rules, and one draw needn't show every extreme that they name: `ancestor_indices`: in every localization tile, the 8 slots s with the same s // 8 take at most 4 parents from any one group of particles with the same p // 8, and exactly 4 from some group.
All inputs are finite; a program needn't handle non-finite values. No bound on the sum of `measured_indicator` on one device may be relied on, other than what follows from the above.
Results may differ from a plain program's by a relative error of at most 0.0085.
Values may be sent and summed in bfloat16 or wider, within the bound.
No kernel may reach another device: no remote copies, remote signals or barrier semaphores. Data moves between devices by JAX's collectives and lax.ppermute only.
A program may use at most 128 MiB of HBM per device.

v0:
```python
import functools

import jax
import jax.numpy as jnp
from jax import lax
from jax.experimental import pallas as pl
from jax.experimental.pallas import tpu as pltpu
from jax.sharding import PartitionSpec as P

PATCH_NORTHWARD = 32
PATCH_EASTWARD = 128
RADIUS = 16


relax_factor = 0.6


def extended(shard, sides, width):
    for axis, dim in sides:
        peers, length = (lax.axis_size(axis), shard.shape[dim])
        up = [(i, (i + 1) % peers) for i in range(peers - 1)]
        down = [(j, i) for i, j in up]
        last = lax.slice_in_dim(shard, length - width, length, axis=dim)
        first = lax.slice_in_dim(shard, 0, width, axis=dim)
        before = lax.ppermute(last, axis, up)
        after = lax.ppermute(first, axis, down)
        shard = jnp.concatenate([before, shard, after], axis=dim)
    return shard


def taper_band(inner_count, radius):
    tap_count = 2 * radius + 1
    offsets = jnp.arange(tap_count, dtype=jnp.float32) - radius
    tap_width = radius / 2.0
    tap_total = jnp.sum(jnp.exp(-0.5 * (offsets / tap_width) ** 2))
    out_index = jnp.arange(inner_count, dtype=jnp.int32)[:, None]
    in_index = jnp.arange(inner_count + 2 * radius, dtype=jnp.int32)[None, :]
    offset_index = in_index - out_index
    inside = (offset_index >= 0) & (offset_index < tap_count)
    shifted = (offset_index - radius).astype(jnp.float32)
    values = jnp.exp(-0.5 * (shifted / tap_width) ** 2) / tap_total
    return jnp.where(inside, values, 0.0)


def expand_patches(values):
    lead = values.shape[:-2]
    rows, cols = (values.shape[-2], values.shape[-1])
    grown = jnp.broadcast_to(values[..., :, None, :, None], lead + (rows, 2, cols, 2))
    return grown.reshape(lead + (rows * 2, cols * 2))


def doubled(values):
    rows, cols = values.shape
    to_rows = lax.broadcasted_iota(jnp.int32, (2 * rows, rows), 0) // 2
    of_rows = lax.broadcasted_iota(jnp.int32, (2 * rows, rows), 1)
    tall = (to_rows == of_rows).astype(jnp.float32)
    of_cols = lax.broadcasted_iota(jnp.int32, (cols, 2 * cols), 0)
    to_cols = lax.broadcasted_iota(jnp.int32, (cols, 2 * cols), 1) // 2
    wide = (to_cols == of_cols).astype(jnp.float32)
    grown = jnp.dot(values, wide, precision=lax.Precision.HIGHEST)
    return jnp.dot(tall, grown, precision=lax.Precision.HIGHEST)


def tiles_of(rows, cols):
    return [
        (north, east)
        for north in range(rows // PATCH_NORTHWARD)
        for east in range(cols // PATCH_EASTWARD)
    ]


def tile_window(north, east):
    return (
        pl.ds(north * PATCH_NORTHWARD, PATCH_NORTHWARD),
        pl.ds(east * PATCH_EASTWARD, PATCH_EASTWARD),
    )


def pick_tiles(ancestors, place, prior_states, targets, seats):
    members, heights, rows, cols = prior_states.shape
    tiles = tiles_of(rows, cols)

    def kernel(ancestor, spot, prior, out, sems):
        own = spot[0]

        def transfer(target, seat, member, tile):
            window = tile_window(*tiles[tile])
            return pltpu.make_async_copy(
                prior.at[(member, slice(None)) + window],
                out.at[(target, seat, slice(None)) + window],
                sems.at[target, seat, tile],
            )

        used = {}
        for target in range(targets):
            for tile in range(len(tiles)):
                rank = jnp.int32(0)
                for slot in range(members):
                    parent = ancestor[(spot[1 + target] * members + slot) * len(tiles) + tile]
                    local = parent - own * members
                    hit = (local >= 0) & (local < members) & (rank < seats)

                    @pl.when(hit)
                    def _(target=target, rank=rank, local=local, tile=tile):
                        transfer(target, rank, local, tile).start()

                    rank = rank + hit.astype(jnp.int32)
                used[target, tile] = rank
        for (target, tile), rank in used.items():
            for seat in range(seats):

                @pl.when(seat < rank)
                def _(target=target, seat=seat, tile=tile):
                    transfer(target, seat, 0, tile).wait()

    return pl.pallas_call(
        kernel,
        out_shape=jax.ShapeDtypeStruct((targets, seats, heights, rows, cols), prior_states.dtype),
        in_specs=[
            pl.BlockSpec(memory_space=pltpu.SMEM),
            pl.BlockSpec(memory_space=pltpu.SMEM),
            pl.BlockSpec(memory_space=pltpu.HBM),
        ],
        out_specs=pl.BlockSpec(memory_space=pltpu.HBM),
        scratch_shapes=[pltpu.SemaphoreType.DMA((targets, seats, len(tiles)))],
        name="pick_tiles",
    )(ancestors, place, prior_states)


def group_mean(log_weight, prior_states, chunk):
    members, heights, rows, cols = prior_states.shape
    pixel_rows, pixel_cols = log_weight.shape[1:]

    def kernel(log_ref, prior, scaled_ref, norm_ref, mean_ref, sent_ref, share):
        @pl.when(pl.program_id(0) == 0)
        def _():
            values = log_ref[...]
            peak = jnp.max(values, axis=0)
            scaled = jnp.exp(values - peak[None])
            total = jnp.sum(scaled, axis=0)
            scaled_ref[...] = scaled
            norm_ref[0] = peak
            norm_ref[1] = total
            for member in range(members):
                share[member] = doubled(scaled[member] / total)

        for level in range(chunk):
            mean = share[0] * prior[0, level].astype(jnp.float32)
            for member in range(1, members):
                mean = mean + share[member] * prior[member, level].astype(jnp.float32)
            mean_ref[level] = mean
            sent_ref[level] = mean.astype(jnp.bfloat16)

    return pl.pallas_call(
        kernel,
        grid=(heights // chunk,),
        out_shape=(
            jax.ShapeDtypeStruct(log_weight.shape, jnp.float32),
            jax.ShapeDtypeStruct((2, pixel_rows, pixel_cols), jnp.float32),
            jax.ShapeDtypeStruct((heights, rows, cols), jnp.float32),
            jax.ShapeDtypeStruct((heights, rows, cols), jnp.bfloat16),
        ),
        in_specs=[
            pl.BlockSpec(log_weight.shape, lambda i: (0, 0, 0)),
            pl.BlockSpec((members, chunk, rows, cols), lambda i: (0, i, 0, 0)),
        ],
        out_specs=(
            pl.BlockSpec(log_weight.shape, lambda i: (0, 0, 0)),
            pl.BlockSpec((2, pixel_rows, pixel_cols), lambda i: (0, 0, 0)),
            pl.BlockSpec((chunk, rows, cols), lambda i: (i, 0, 0)),
            pl.BlockSpec((chunk, rows, cols), lambda i: (i, 0, 0)),
        ),
        scratch_shapes=[pltpu.VMEM((members, rows, cols), jnp.float32)],
        compiler_params=pltpu.CompilerParams(vmem_limit_bytes=32 << 20),
        name="group_mean",
    )(log_weight, prior_states)


def combine(ancestors, place, scaled, own_norm, other_norm, own_mean, other_mean, prior_states, received, chunk, shared):
    members, heights, rows, cols = prior_states.shape
    tiles = tiles_of(rows, cols)
    count = len(tiles)
    groups = ancestors.shape[0] // (members * count)
    sources, seats = received.shape[:2]
    received = received.reshape((sources * seats,) + received.shape[2:])
    steps = heights // chunk

    def kernel(
        ancestor, spot, scaled_ref, own_ref, other_ref, mean_ref, peer_ref, prior, remote,
        out, weights, picks, own_share, other_share, table, seen, sems,
    ):
        step = pl.program_id(0)

        def transfer(array, source, at, slot, tile, half):
            window = tile_window(*tiles[tile])
            levels = pl.ds(at * chunk, chunk)
            return pltpu.make_async_copy(
                array.at[(source, levels) + window],
                picks.at[(half, slot, slice(None)) + window],
                sems.at[half, slot, tile],
            )

        def fetch(at, half):
            for slot in range(members):
                for tile in range(count):
                    source = table[slot * count + tile]

                    @pl.when(source < members)
                    def _():
                        transfer(prior, source, at, slot, tile, half).start()

                    @pl.when(source >= members)
                    def _():
                        transfer(remote, source - members, at, slot, tile, half).start()

        @pl.when(step == 0)
        def _():
            own = spot[0]
            for tile in range(count):
                for group in range(groups):
                    seen[group] = 0
                for slot in range(members):
                    parent = ancestor[(own * members + slot) * count + tile]
                    group = lax.div(parent, jnp.int32(members))
                    rank = seen[group]
                    seen[group] = rank + 1
                    line = (jnp.int32(0) if sources == 1 else group) * seats + rank
                    table[slot * count + tile] = jnp.where(
                        group == own, parent - own * members, members + line
                    )
            fetch(0, 0)
            own_peak, own_total = own_ref[0], own_ref[1]
            other_peak, other_total = other_ref[0], other_ref[1]
            peak = jnp.maximum(own_peak, other_peak)
            own_scale = jnp.exp(own_peak - peak)
            if shared:
                total = other_total
            else:
                other_part = other_total * jnp.exp(other_peak - peak)
                total = own_total * own_scale + other_part
                own_share[...] = (1.0 - relax_factor) * doubled(own_total * own_scale / total)
                other_share[...] = (1.0 - relax_factor) * doubled(other_part / total)
            weights[...] = scaled_ref[...] * (own_scale / total)[None]

        @pl.when(step + 1 < steps)
        def _():
            fetch(step + 1, lax.rem(step + 1, 2))

        half = lax.rem(step, 2)
        for slot in range(members):
            for tile in range(count):
                transfer(prior, 0, 0, slot, tile, half).wait()
        for level in range(chunk):
            if shared:
                base = (1.0 - relax_factor) * mean_ref[level]
            else:
                base = own_share[...] * mean_ref[level] + other_share[...] * peer_ref[
                    level
                ].astype(jnp.float32)
            for slot in range(members):
                out[slot, level] = base + relax_factor * picks[half, slot, level].astype(
                    jnp.float32
                )

    small = lambda i: (0, 0, 0)
    return pl.pallas_call(
        kernel,
        grid=(steps,),
        out_shape=(
            jax.ShapeDtypeStruct(prior_states.shape, jnp.float32),
            jax.ShapeDtypeStruct(scaled.shape, jnp.float32),
        ),
        in_specs=[
            pl.BlockSpec(memory_space=pltpu.SMEM),
            pl.BlockSpec(memory_space=pltpu.SMEM),
            pl.BlockSpec(scaled.shape, small),
            pl.BlockSpec(own_norm.shape, small),
            pl.BlockSpec(other_norm.shape, small),
            pl.BlockSpec((chunk, rows, cols), lambda i: (i, 0, 0)),
            pl.BlockSpec((chunk, rows, cols), lambda i: (i, 0, 0)),
            pl.BlockSpec(memory_space=pltpu.HBM),
            pl.BlockSpec(memory_space=pltpu.HBM),
        ],
        out_specs=(
            pl.BlockSpec((members, chunk, rows, cols), lambda i: (0, i, 0, 0)),
            pl.BlockSpec(scaled.shape, small),
        ),
        scratch_shapes=[
            pltpu.VMEM((2, members, chunk, rows, cols), prior_states.dtype),
            pltpu.VMEM((rows, cols), jnp.float32),
            pltpu.VMEM((rows, cols), jnp.float32),
            pltpu.SMEM((members * count,), jnp.int32),
            pltpu.SMEM((groups,), jnp.int32),
            pltpu.SemaphoreType.DMA((2, members, count)),
        ],
        compiler_params=pltpu.CompilerParams(vmem_limit_bytes=32 << 20),
        name="combine",
    )(
        ancestors, place, scaled, own_norm, other_norm, own_mean, other_mean, prior_states, received
    )


def log_weights(
    prior_states,
    measured_brightness,
    measured_indicator,
    sensor_error_spread,
    entry_layer_stencil,
    entry_layer_offset,
    middle_layer_stencil,
    middle_layer_offset,
    brightness_matrix,
    brightness_offset,
):
    numbers = ("NCHW", "OIHW", "NCHW")
    highest = lax.Precision.HIGHEST
    enlarged_state = extended(prior_states, (("lat", 2), ("lon", 3)), 2)
    first_layer = lax.conv_general_dilated(
        enlarged_state,
        entry_layer_stencil,
        (2, 2),
        "VALID",
        dimension_numbers=numbers,
        preferred_element_type=jnp.float32,
    )
    first_layer = jax.nn.relu(first_layer + entry_layer_offset[None, :, None, None]).astype(
        jnp.bfloat16
    )
    first_wide = extended(first_layer, (("lat", 2), ("lon", 3)), 2)
    second_layer = lax.conv_general_dilated(
        first_wide,
        middle_layer_stencil,
        (1, 1),
        "VALID",
        rhs_dilation=(2, 2),
        dimension_numbers=numbers,
        preferred_element_type=jnp.float32,
    )
    second_layer = jax.nn.relu(second_layer + middle_layer_offset[None, :, None, None]).astype(
        jnp.bfloat16
    )
    predicted = (
        jnp.einsum(
            "oc,pcij->poij", brightness_matrix, second_layer, preferred_element_type=jnp.float32
        )
        + brightness_offset[None, :, None, None]
    )
    innovation = measured_brightness[None] - predicted
    departure_power_two = (
        jnp.sum(innovation * innovation / sensor_error_spread[None, :, None, None], axis=1)
        * measured_indicator.astype(jnp.float32)[None]
    )
    band_lat = taper_band(departure_power_two.shape[1], RADIUS)
    band_lon = taper_band(departure_power_two.shape[2], RADIUS)
    padded = extended(departure_power_two, (("lat", 1),), RADIUS)
    lat_smooth = jnp.einsum("ij,pjk->pik", band_lat, padded, precision=highest)
    lat_smooth = extended(lat_smooth, (("lon", 2),), RADIUS)
    smooth = jnp.einsum("pij,kj->pik", lat_smooth, band_lon, precision=highest)
    return -0.5 * smooth


def chunk_of(heights):
    return next(size for size in (5, 4, 2, 1) if heights % size == 0)


def body(prior_states, *rest):
    ancestor_indices = rest[-1]
    members, heights, rows, cols = prior_states.shape
    groups = lax.axis_size("ens")
    own = lax.axis_index("ens").astype(jnp.int32)
    seats = max(2, (members + groups - 1) // groups)
    ancestors = ancestor_indices.reshape(-1)
    swap = [(0, 1), (1, 0)]
    paired = groups == 2
    if paired:
        targets = (1 - own)[None]
    else:
        targets = jnp.arange(groups, dtype=jnp.int32)
    place = jnp.concatenate([own[None], targets])
    outgoing = pick_tiles(ancestors, place, prior_states, targets.shape[0], seats)
    if paired:
        received = lax.ppermute(outgoing, "ens", swap)
    else:
        received = lax.all_to_all(outgoing, "ens", split_axis=0, concat_axis=0, tiled=True)
    log_weight = log_weights(prior_states, *rest[:-1])
    scaled, own_norm, own_mean, sent_mean = group_mean(
        log_weight, prior_states, chunk_of(heights)
    )
    if paired:
        other_norm = lax.ppermute(own_norm, "ens", swap)
        other_mean = lax.ppermute(sent_mean, "ens", swap)
    else:
        peak = lax.pmax(own_norm[0], "ens")
        part = own_norm[1] * jnp.exp(own_norm[0] - peak)
        total, own_mean = lax.psum((part, expand_patches(part)[None] * own_mean), "ens")
        own_mean = own_mean / expand_patches(total)[None]
        other_norm = jnp.stack([peak, total])
        other_mean = sent_mean
    return combine(
        ancestors,
        place,
        scaled,
        own_norm,
        other_norm,
        own_mean,
        other_mean,
        prior_states,
        received,
        chunk_of(heights),
        not paired,
    )


def solution(mesh):
    return jax.shard_map(
        body,
        mesh=mesh,
        in_specs=(
            P("ens", None, "lat", "lon"),
            P(None, "lat", "lon"),
            P("lat", "lon"),
            P(),
            P(),
            P(),
            P(),
            P(),
            P(),
            P(),
            P(None, "lat", "lon"),
        ),
        out_specs=(P("ens", None, "lat", "lon"), P("ens", "lat", "lon")),
        check_vma=False,
    )
```

profile of v0, /device:TPU:0, one launch (start us, length us, event | category | flops | bytes accessed | tf_op | source)
XLA Modules:
  0.0 262.4 jit_solution(11757945445756524120)
XLA Ops:
  0.6 0.0 copy-start
  0.6 2.3 fusion.109
  3.0 4.9 %collective-permute-start = (bf16[8,40,2,256]{3,1,2,0:T(8,128)(2,1)S(1)}, bf16[8,40,2,256]{3,1,2,0:T(8,128)(2,1)S(1)}, u32[]{:S(2)}, u32[]{:S(2)}) collective-permute-start(bf16[8,40,2,256]{3,1,2,0:T(8,128)(2,1)S(1)} %copy.52), channel_id=1, source_target_pairs={{0,4},{4,8},{8,12},{1,5},{5,9},{9,13},{2,6},{6,10},{10,14},{3,7},{... | collective-permute-start | bytes 983048 | tf_op jit(solution)/shard_map/ppermute | solution.py:25
  8.0 1.3 collective-permute-start.1
  9.3 14.0 %copy.48 = bf16[8,40,32,256]{1,0,3,2:T(8,128)(2,1)} copy(bf16[8,40,32,256]{3,2,1,0:T(8,128)(2,1)} %prior.5) | data formatting | bytes 10485760 | tf_op args[0]
  23.2 0.6 copy.47
  23.8 1.5 copy.49
  25.4 1.1 pad_maximum_fusion.2
  26.4 1.5 collective-permute-start.2
  27.9 1.3 collective-permute-start.3
  29.2 3.7 %collective-permute-done.3 = bf16[8,40,36,2]{1,0,3,2:T(8,128)(2,1)} collective-permute-done((bf16[8,40,36,2]{1,0,3,2:T(8,128)(2,1)S(1)}, bf16[8,40,36,2]{1,0,3,2:T(8,128)(2,1)}, u32[]{:S(2)}, u32[]{:S(2)}) %collective-permute-start.3) | collective-permute-done | bytes 46112 | tf_op jit(solution)/shard_map/ppermute | solution.py:26
  32.9 36.2 %maximum_convert_fusion.1 = bf16[8,64,16,128]{1,0,3,2:T(8,128)(2,1)S(1)} fusion(f32[64]{0:T(128)S(1)} %copy-done.9, bf16[64,40,5,5]{0,1,3,2:T(8,128)(2,1)S(1)} %copy-done, bf16[8,40,36,2]{1,0,3,2:T(8,128)(2,1)} %collective-permute-done.3, bf16[8,40,2,256]{1,0,3,2:T(8,128)(2,1)S(1)} %copy.49, bf16[8,40,32,256]{1,0,3,2:T(8,128)(2,1)} %copy.48, ...), kind=kOutput, calls=%fused_computation.11 | convolution fusion | flops 2112278528 | bytes 8215808 | tf_op jit(solution)/shard_map/conv_general_dilated | solution.py:318
  69.1 2.0 copy-done.3
  71.1 0.1 fusion.110
  71.1 4.6 %collective-permute-start.4 = (bf16[8,64,2,128]{1,0,3,2:T(8,128)(2,1)S(1)}, bf16[8,64,2,128]{1,0,3,2:T(8,128)(2,1)S(1)}, u32[]{:S(2)}, u32[]{:S(2)}) collective-permute-start(bf16[8,64,2,128]{1,0,3,2:T(8,128)(2,1)S(1)} %get-tuple-element.16), channel_id=1, source_target_pairs={{0,4},{4,8},{8,12},{1,5},{5,9},{9,13},{2,6},{6,10},{10,14},{3,7},{... | collective-permute-start | bytes 786440 | tf_op jit(solution)/shard_map/ppermute | solution.py:25
  75.7 1.5 collective-permute-start.5
  77.2 8.0 %collective-permute-done.4 = bf16[8,64,2,128]{1,0,3,2:T(8,128)(2,1)S(1)} collective-permute-done((bf16[8,64,2,128]{1,0,3,2:T(8,128)(2,1)S(1)}, bf16[8,64,2,128]{1,0,3,2:T(8,128)(2,1)S(1)}, u32[]{:S(2)}, u32[]{:S(2)}) %collective-permute-start.4) | collective-permute-done | bytes 262176 | tf_op jit(solution)/shard_map/ppermute | solution.py:25
  85.2 4.7 %collective-permute-done.5 = bf16[8,64,2,128]{1,0,3,2:T(8,128)(2,1)S(1)} collective-permute-done((bf16[8,64,2,128]{1,0,3,2:T(8,128)(2,1)S(1)}, bf16[8,64,2,128]{1,0,3,2:T(8,128)(2,1)S(1)}, u32[]{:S(2)}, u32[]{:S(2)}) %collective-permute-start.5) | collective-permute-done | bytes 262176 | tf_op jit(solution)/shard_map/ppermute | solution.py:26
  89.9 0.9 pad_maximum_fusion.5
  90.9 0.0 copy-start.10
  90.9 4.3 %collective-permute-start.6 = (bf16[8,64,20,2]{1,0,3,2:T(8,128)(2,1)S(1)}, bf16[8,64,20,2]{1,0,3,2:T(8,128)(2,1)S(1)}, u32[]{:S(2)}, u32[]{:S(2)}) collective-permute-start(bf16[8,64,20,2]{1,0,3,2:T(8,128)(2,1)S(1)} %get-tuple-element.12), channel_id=1, source_target_pairs={{0,1},{1,2},{2,3},{4,5},{5,6},{6,7},{8,9},{9,10},{10,11},{12,13},{... | collective-permute-start | bytes 122888 | tf_op jit(solution)/shard_map/ppermute | solution.py:25
  95.2 1.3 collective-permute-start.7
  96.5 0.6 pad_add_fusion.spot
  97.1 0.1 copy.43
  97.2 0.6 reshape.16.ancestor
  97.8 81.4 %pick_tiles.1 = bf16[1,4,40,32,256]{4,3,2,1,0:T(8,128)(2,1)} custom-call(s32[32]{0:T(128)} %reshape.16.ancestor, s32[2]{0:T(128)} %pad_add_fusion.spot, bf16[8,40,32,256]{3,2,1,0:T(8,128)(2,1)} %prior.5), custom_call_target="tpu_custom_call" | custom-call | tf_op jit(solution)/shard_map/pick_tiles/pallas_call | solution.py:116
  179.2 1.6 collective-permute-start.14
  180.9 0.0 copy-start.8
  180.9 0.0 slice-start.1
  181.0 13.4 %maximum_convert_fusion = bf16[8,64,16,128]{1,0,3,2:T(8,128)(2,1)S(1)} fusion(f32[64]{0:T(128)S(1)} %copy-done.10, bf16[64,64,3,3]{1,0,3,2:T(8,128)(2,1)S(1)} %copy-done.7, bf16[8,64,20,2]{1,0,3,2:T(8,128)(2,1)S(1)} %collective-permute-done.7, bf16[8,64,2,128]{1,0,3,2:T(8,128)(2,1)S(1)} %collective-permute-done.5, bf16[8,64,16,128]{1,0,3,2:T(8,128)(2,1)} %copy-done.3, ...), kind=kOutput, calls=%fused_computation.10 | convolution fusion | flops 1216512000 | bytes 4874496 | tf_op jit(solution)/shard_map/conv_general_dilated | solution.py:330
  194.5 1.3 divide_reduce_fusion
  195.7 0.0 copy-start.1
  195.8 3.7 %collective-permute-start.8 = (f32[8,16,128]{2,1,0:T(8,128)S(1)}, f32[8,16,128]{2,1,0:T(8,128)S(1)}, u32[]{:S(2)}, u32[]{:S(2)}) collective-permute-start(f32[8,16,128]{2,1,0:T(8,128)S(1)} %broadcast_multiply_fusion), channel_id=1, source_target_pairs={{0,4},{4,8},{8,12},{1,5},{5,9},{9,13},{2,6},{6,10},{10,14},{3,7},{... | collective-permute-start | bytes 196616 | tf_op jit(solution)/shard_map/ppermute | solution.py:25
  199.5 1.3 collective-permute-start.9
  200.8 0.6 exponential_reduce_fusion
  201.4 0.4 collective-permute-done.8
  201.9 4.4 %collective-permute-done.9 = f32[8,16,128]{2,1,0:T(8,128)S(1)} collective-permute-done((f32[8,16,128]{2,1,0:T(8,128)S(1)}, f32[8,16,128]{2,1,0:T(8,128)S(1)}, u32[]{:S(2)}, u32[]{:S(2)}) %collective-permute-start.9) | collective-permute-done | bytes 65568 | tf_op jit(solution)/shard_map/ppermute | solution.py:26
  206.2 0.9 convolution_bitcast_fusion
  207.1 0.1 fusion.111
  207.2 1.9 collective-permute-start.10
  209.1 1.3 collective-permute-start.11
  210.4 3.2 %collective-permute-done.11 = f32[8,16,16]{2,1,0:T(8,128)S(1)} collective-permute-done((f32[8,16,16]{2,1,0:T(8,128)S(1)}, f32[8,16,16]{2,1,0:T(8,128)S(1)}, u32[]{:S(2)}, u32[]{:S(2)}) %collective-permute-start.11) | collective-permute-done | bytes 8224 | tf_op jit(solution)/shard_map/ppermute | solution.py:26
  213.6 1.0 convolution_multiply_fusion.log_ref
  214.5 3.7 %group_mean.1 = (f32[8,16,128]{2,1,0:T(8,128)S(1)}, f32[2,16,128]{2,1,0:T(8,128)S(1)}, f32[40,32,256]{2,1,0:T(8,128)S(1)}, bf16[40,32,256]{2,1,0:T(8,128)(2,1)S(1)}) custom-call(f32[8,16,128]{2,1,0:T(8,128)S(1)} %convolution_multiply_fusion.log_ref, bf16[8,40,32,256]{3,2,1,0:T(8,128)(2,1)S(1)} %bitcast.29), custom_call_target="tpu_custom_call" | custom-call | tf_op jit(solution)/shard_map/group_mean/pallas_call | solution.py:154
  218.2 0.6 collective-permute-start.13
  218.8 1.5 collective-permute-start.12
  220.3 33.2 %collective-permute-done.12.other_ref = f32[2,16,128]{2,1,0:T(8,128)S(1)} collective-permute-done((f32[2,16,128]{2,1,0:T(8,128)S(1)}, f32[2,16,128]{2,1,0:T(8,128)S(1)}, u32[]{:S(2)}, u32[]{:S(2)}) %collective-permute-start.12) | collective-permute-done | bytes 16416 | tf_op jit(solution)/shard_map/ppermute | solution.py:390
  253.5 8.7 %combine.1 = (f32[8,40,32,256]{3,2,1,0:T(8,128)}, f32[8,16,128]{2,1,0:T(8,128)}) custom-call(s32[32]{0:T(128)S(1)} %copy-done.1, s32[2]{0:T(128)S(1)} %copy-done.2, f32[8,16,128]{2,1,0:T(8,128)S(1)} %get-tuple-element.6.scaled_ref, f32[2,16,128]{2,1,0:T(8,128)S(1)} %get-tuple-element.7.own_ref, f32[2,16,128]{2,1,0:T(8,128)S(1)} %collective-permute-done.12.other_ref, ...), custom_call_target="tpu_custom_call" | custom-call | tf_op jit(solution)/shard_map/combine/pallas_call | solution.py:266
  (38 shorter events, 0.2 us)
Async XLA Ops:
  0.6 32.2 %copy-start = (bf16[64,40,5,5]{0,1,3,2:T(8,128)(2,1)S(1)}, bf16[64,40,5,5]{0,1,3,2:T(8,128)(2,1)}, u32[]{:S(2)}) copy-start(bf16[64,40,5,5]{0,1,3,2:T(8,128)(2,1)} %param.15) | copy-start | bytes 384004
  3.0 20.3 %collective-permute-start = (bf16[8,40,2,256]{3,1,2,0:T(8,128)(2,1)S(1)}, bf16[8,40,2,256]{3,1,2,0:T(8,128)(2,1)S(1)}, u32[]{:S(2)}, u32[]{:S(2)}) collective-permute-start(bf16[8,40,2,256]{3,1,2,0:T(8,128)(2,1)S(1)} %copy.52), channel_id=1, source_target_pairs={{0,4},{4,8},{8,12},{1,5},{5,9},{9,13},{2,6},{6,10},{10,14},{3,7},{... | collective-permute-start | bytes 983048 | tf_op jit(solution)/shard_map/ppermute | solution.py:25
  8.0 15.8 %collective-permute-start.1 = (bf16[8,40,2,256]{3,1,2,0:T(8,128)(2,1)S(1)}, bf16[8,40,2,256]{3,1,2,0:T(8,128)(2,1)}, u32[]{:S(2)}, u32[]{:S(2)}) collective-permute-start(bf16[8,40,2,256]{3,1,2,0:T(8,128)(2,1)S(1)} %copy.53), channel_id=1, source_target_pairs={{4,0},{8,4},{12,8},{5,1},{9,5},{13,9},{6,2},{10,6},{14,10},{7,3},{... | collective-permute-start | bytes 983048 | tf_op jit(solution)/shard_map/ppermute | solution.py:26
  25.4 7.5 %copy-start.9 = (f32[64]{0:T(128)S(1)}, f32[64]{0:T(128)}, u32[]{:S(2)}) copy-start(f32[64]{0:T(128)} %param.16) | copy-start | bytes 772
  26.4 2.8 %collective-permute-start.2 = (bf16[8,40,36,2]{1,0,3,2:T(8,128)(2,1)S(1)}, bf16[8,40,36,2]{1,0,3,2:T(8,128)(2,1)S(1)}, u32[]{:S(2)}, u32[]{:S(2)}) collective-permute-start(bf16[8,40,36,2]{1,0,3,2:T(8,128)(2,1)S(1)} %get-tuple-element.10), channel_id=1, source_target_pairs={{0,1},{1,2},{2,3},{4,5},{5,6},{6,7},{8,9},{9,10},{10,11},{12,13},{... | collective-permute-start | bytes 138248 | tf_op jit(solution)/shard_map/ppermute | solution.py:25
  27.9 5.0 %collective-permute-start.3 = (bf16[8,40,36,2]{1,0,3,2:T(8,128)(2,1)S(1)}, bf16[8,40,36,2]{1,0,3,2:T(8,128)(2,1)}, u32[]{:S(2)}, u32[]{:S(2)}) collective-permute-start(bf16[8,40,36,2]{1,0,3,2:T(8,128)(2,1)S(1)} %get-tuple-element.11), channel_id=1, source_target_pairs={{1,0},{2,1},{3,2},{5,4},{6,5},{7,6},{9,8},{10,9},{11,10},{13,12},{... | collective-permute-start | bytes 138248 | tf_op jit(solution)/shard_map/ppermute | solution.py:26
  69.0 2.0 copy-start.3
  71.1 26.1 %copy-start.6 = (s32[16,1,2]{0,2,1:T(2,128)S(1)}, s32[16,1,2]{0,2,1:T(2,128)}, u32[]{:S(2)}) copy-start(s32[16,1,2]{0,2,1:T(2,128)} %param.21) | copy-start | bytes 388
  71.1 14.1 %collective-permute-start.4 = (bf16[8,64,2,128]{1,0,3,2:T(8,128)(2,1)S(1)}, bf16[8,64,2,128]{1,0,3,2:T(8,128)(2,1)S(1)}, u32[]{:S(2)}, u32[]{:S(2)}) collective-permute-start(bf16[8,64,2,128]{1,0,3,2:T(8,128)(2,1)S(1)} %get-tuple-element.16), channel_id=1, source_target_pairs={{0,4},{4,8},{8,12},{1,5},{5,9},{9,13},{2,6},{6,10},{10,14},{3,7},{... | collective-permute-start | bytes 786440 | tf_op jit(solution)/shard_map/ppermute | solution.py:25
  75.7 14.2 %collective-permute-start.5 = (bf16[8,64,2,128]{1,0,3,2:T(8,128)(2,1)S(1)}, bf16[8,64,2,128]{1,0,3,2:T(8,128)(2,1)S(1)}, u32[]{:S(2)}, u32[]{:S(2)}) collective-permute-start(bf16[8,64,2,128]{1,0,3,2:T(8,128)(2,1)S(1)} %get-tuple-element.17), channel_id=1, source_target_pairs={{4,0},{8,4},{12,8},{5,1},{9,5},{13,9},{6,2},{10,6},{14,10},{7,3},{... | collective-permute-start | bytes 786440 | tf_op jit(solution)/shard_map/ppermute | solution.py:26
  77.2 103.6 %copy-start.4 = (f32[16,16,128]{2,1,0:T(8,128)S(1)}, f32[16,16,128]{2,1,0:T(8,128)}, u32[]{:S(2)}) copy-start(f32[16,16,128]{2,1,0:T(8,128)} %param.12) | copy-start | bytes 393220
  90.8 90.0 %copy-start.5 = (s32[16,128]{1,0:T(8,128)S(1)}, s32[16,128]{1,0:T(8,128)}, u32[]{:S(2)}) copy-start(s32[16,128]{1,0:T(8,128)} %param.13) | copy-start | bytes 24580
  90.9 90.1 %copy-start.7 = (bf16[64,64,3,3]{1,0,3,2:T(8,128)(2,1)S(1)}, bf16[64,64,3,3]{1,0,3,2:T(8,128)(2,1)}, u32[]{:S(2)}) copy-start(bf16[64,64,3,3]{1,0,3,2:T(8,128)(2,1)} %param.17) | copy-start | bytes 221188
  90.9 90.1 %copy-start.10 = (f32[64]{0:T(128)S(1)}, f32[64]{0:T(128)}, u32[]{:S(2)}) copy-start(f32[64]{0:T(128)} %param.18) | copy-start | bytes 772
  90.9 90.1 %collective-permute-start.6 = (bf16[8,64,20,2]{1,0,3,2:T(8,128)(2,1)S(1)}, bf16[8,64,20,2]{1,0,3,2:T(8,128)(2,1)S(1)}, u32[]{:S(2)}, u32[]{:S(2)}) collective-permute-start(bf16[8,64,20,2]{1,0,3,2:T(8,128)(2,1)S(1)} %get-tuple-element.12), channel_id=1, source_target_pairs={{0,1},{1,2},{2,3},{4,5},{5,6},{6,7},{8,9},{9,10},{10,11},{12,13},{... | collective-permute-start | bytes 122888 | tf_op jit(solution)/shard_map/ppermute | solution.py:25
  95.2 85.7 %collective-permute-start.7 = (bf16[8,64,20,2]{1,0,3,2:T(8,128)(2,1)S(1)}, bf16[8,64,20,2]{1,0,3,2:T(8,128)(2,1)S(1)}, u32[]{:S(2)}, u32[]{:S(2)}) collective-permute-start(bf16[8,64,20,2]{1,0,3,2:T(8,128)(2,1)S(1)} %get-tuple-element.13), channel_id=1, source_target_pairs={{1,0},{2,1},{3,2},{5,4},{6,5},{7,6},{9,8},{10,9},{11,10},{13,12},{... | collective-permute-start | bytes 122888 | tf_op jit(solution)/shard_map/ppermute | solution.py:26
  97.8 116.7 %slice-start = ((s8[5242880]{0:T(1024)(128)(4,1)}), s8[1048576]{0:T(1024)(128)(4,1)S(1)}, s32[]{:S(2)}) async-start(s8[5242880]{0:T(1024)(128)(4,1)} %bitcast.28), calls=%async_computation | async-start | bytes 2097152
  179.2 74.3 %collective-permute-start.14 = (bf16[1,4,40,32,256]{4,3,2,1,0:T(8,128)(2,1)}, bf16[1,4,40,32,256]{4,3,2,1,0:T(8,128)(2,1)S(1)}, u32[]{:S(2)}, u32[]{:S(2)}) collective-permute-start(bf16[1,4,40,32,256]{4,3,2,1,0:T(8,128)(2,1)} %pick_tiles.1), channel_id=1, source_target_pairs={{0,16},{16,0},{1,17},{17,1},{2,18},{18,2},{3,19},{19,3},{4,20},{20... | collective-permute-start | bytes 7864328 | tf_op jit(solution)/shard_map/ppermute | solution.py:382
  180.9 13.5 %copy-start.8 = (bf16[16,64]{1,0:T(8,128)(2,1)S(1)}, bf16[16,64]{1,0:T(8,128)(2,1)}, u32[]{:S(2)}) copy-start(bf16[16,64]{1,0:T(8,128)(2,1)} %param.19) | copy-start | bytes 6148
  180.9 13.5 %copy-start.11 = (f32[16]{0:T(128)S(1)}, f32[16]{0:T(128)}, u32[]{:S(2)}) copy-start(f32[16]{0:T(128)} %param.14) | copy-start | bytes 196
  180.9 13.5 %copy-start.12 = (f32[16]{0:T(128)S(1)}, f32[16]{0:T(128)}, u32[]{:S(2)}) copy-start(f32[16]{0:T(128)} %param.20) | copy-start | bytes 196
  180.9 33.6 %slice-start.1 = ((s8[5242880]{0:T(1024)(128)(4,1)}), s8[4194304]{0:T(1024)(128)(4,1)S(1)}, s32[]{:S(2)}) async-start(s8[5242880]{0:T(1024)(128)(4,1)} %bitcast.28), calls=%async_computation.1 | async-start | bytes 8388608
  195.7 57.8 %copy-start.1 = (s32[32]{0:T(128)S(1)}, s32[32]{0:T(128)}, u32[]{:S(2)}) copy-start(s32[32]{0:T(128)} %reshape.16.ancestor) | copy-start | bytes 388
  195.8 57.7 %copy-start.2 = (s32[2]{0:T(128)S(1)}, s32[2]{0:T(128)}, u32[]{:S(2)}) copy-start(s32[2]{0:T(128)} %pad_add_fusion.spot) | copy-start | bytes 28
  195.8 6.1 %collective-permute-start.8 = (f32[8,16,128]{2,1,0:T(8,128)S(1)}, f32[8,16,128]{2,1,0:T(8,128)S(1)}, u32[]{:S(2)}, u32[]{:S(2)}) collective-permute-start(f32[8,16,128]{2,1,0:T(8,128)S(1)} %broadcast_multiply_fusion), channel_id=1, source_target_pairs={{0,4},{4,8},{8,12},{1,5},{5,9},{9,13},{2,6},{6,10},{10,14},{3,7},{... | collective-permute-start | bytes 196616 | tf_op jit(solution)/shard_map/ppermute | solution.py:25
  199.5 6.7 %collective-permute-start.9 = (f32[8,16,128]{2,1,0:T(8,128)S(1)}, f32[8,16,128]{2,1,0:T(8,128)S(1)}, u32[]{:S(2)}, u32[]{:S(2)}) collective-permute-start(f32[8,16,128]{2,1,0:T(8,128)S(1)} %broadcast_multiply_fusion), channel_id=1, source_target_pairs={{4,0},{8,4},{12,8},{5,1},{9,5},{13,9},{6,2},{10,6},{14,10},{7,3},{... | collective-permute-start | bytes 196616 | tf_op jit(solution)/shard_map/ppermute | solution.py:26
  207.2 3.2 %collective-permute-start.10 = (f32[8,16,16]{2,1,0:T(8,128)S(1)}, f32[8,16,16]{2,1,0:T(8,128)S(1)}, u32[]{:S(2)}, u32[]{:S(2)}) collective-permute-start(f32[8,16,16]{2,1,0:T(8,128)S(1)} %get-tuple-element.18), channel_id=1, source_target_pairs={{0,1},{1,2},{2,3},{4,5},{5,6},{6,7},{8,9},{9,10},{10,11},{12,13},{... | collective-permute-start | bytes 24584 | tf_op jit(solution)/shard_map/ppermute | solution.py:25
  209.1 4.5 %collective-permute-start.11 = (f32[8,16,16]{2,1,0:T(8,128)S(1)}, f32[8,16,16]{2,1,0:T(8,128)S(1)}, u32[]{:S(2)}, u32[]{:S(2)}) collective-permute-start(f32[8,16,16]{2,1,0:T(8,128)S(1)} %get-tuple-element.19), channel_id=1, source_target_pairs={{1,0},{2,1},{3,2},{5,4},{6,5},{7,6},{9,8},{10,9},{11,10},{13,12},{... | collective-permute-start | bytes 24584 | tf_op jit(solution)/shard_map/ppermute | solution.py:26
  218.2 35.3 %collective-permute-start.13 = (bf16[40,32,256]{2,1,0:T(8,128)(2,1)S(1)}, bf16[40,32,256]{2,1,0:T(8,128)(2,1)S(1)}, u32[]{:S(2)}, u32[]{:S(2)}) collective-permute-start(bf16[40,32,256]{2,1,0:T(8,128)(2,1)S(1)} %get-tuple-element.9), channel_id=1, source_target_pairs={{0,16},{16,0},{1,17},{17,1},{2,18},{18,2},{3,19},{19,3},{4,20},{20... | collective-permute-start | bytes 1966088 | tf_op jit(solution)/shard_map/ppermute | solution.py:391
  218.8 34.7 %collective-permute-start.12 = (f32[2,16,128]{2,1,0:T(8,128)S(1)}, f32[2,16,128]{2,1,0:T(8,128)S(1)}, u32[]{:S(2)}, u32[]{:S(2)}) collective-permute-start(f32[2,16,128]{2,1,0:T(8,128)S(1)} %get-tuple-element.7.own_ref), channel_id=1, source_target_pairs={{0,16},{16,0},{1,17},{17,1},{2,18},{18,2},{3,19},{19,3},{4,20},{20... | collective-permute-start | bytes 49160 | tf_op jit(solution)/shard_map/ppermute | solution.py:390
where the time goes:
time: 263 us; the launch traced here: 262 us
  Pallas kernels  93.8 us (36%)
  waiting for transfers between devices  57.6 us (22%)
  matrix products  52.7 us (20%)
  starting transfers between devices  32.5 us (12%)
  local copies, waits for them, and re-layouts  21.4 us (8%)
  other arithmetic  3.2 us (1%)
    pallas_call x1, Pallas kernels, pick_tiles(): pl.pallas_call(kernel, out_shape=jax.ShapeDtypeStruct((targets, seats, he...  81.4 us
    conv_general_dilated x1, matrix products, log_weights(): lax.conv_general_dilated(enlarged_state, entry_layer_stencil, (2, 2), 'VA...  36.2 us
    ppermute x1, waiting for transfers between devices, body(): other_norm = lax.ppermute(own_norm, 'ens', swap)  33.2 us
    ppermute x6, starting transfers between devices, extended(): before = lax.ppermute(last, axis, up)  20.9 us
    unnamed x35, local copies, waits for them, and re-layouts  16.2 us
    ppermute x6, waiting for transfers between devices, extended(): after = lax.ppermute(first, axis, down)  15.9 us
    conv_general_dilated x1, matrix products, log_weights(): lax.conv_general_dilated(first_wide, middle_layer_stencil, (1, 1), 'VALID...  13.4 us
    pallas_call x1, Pallas kernels, combine(): pl.pallas_call(kernel, grid=(steps,), out_shape=(jax.ShapeDtypeStruct(pri...  8.7 us
  transfers between devices with their start and end apart: 15, of which 7 were waited for; matrix products, arithmetic and copies ran while one was open for 13% of the time, Pallas kernels for 32%

commit v1 on v0

--- a/solution.py
+++ b/solution.py
@@ -121,8 +121,9 @@
             pl.BlockSpec(memory_space=pltpu.SMEM),
             pl.BlockSpec(memory_space=pltpu.HBM),
         ],
-        out_specs=pl.BlockSpec(memory_space=pltpu.HBM),
+        out_specs=pl.BlockSpec(memory_space=pltpu.VMEM),
         scratch_shapes=[pltpu.SemaphoreType.DMA((targets, seats, len(tiles)))],
+        compiler_params=pltpu.CompilerParams(vmem_limit_bytes=32 << 20),
         name="pick_tiles",
     )(ancestors, place, prior_states)
 
@@ -300,7 +301,280 @@
     )
 
 
-def log_weights(
+SLOTS = 3
+
+
+def entry_layer(prior_states, even_taps, odd_taps):
+    members, heights, rows, cols = prior_states.shape
+    channels = odd_taps.shape[0] // 2
+    padded = even_taps.shape[1] // 5
+    pixel_rows, pixel_cols = rows // 2, cols // 2
+
+    def kernel(prior, even_ref, odd_ref, out, east_ref, west_ref, sorted_cells, lines):
+        @pl.when(pl.program_id(0) == 0)
+        def _():
+            lines[...] = jnp.zeros_like(lines)
+
+        here = lax.broadcasted_iota(jnp.int32, (cols, cols), 0)
+        there = lax.broadcasted_iota(jnp.int32, (cols, cols), 1)
+        chosen = jnp.where(there < pixel_cols, 2 * there, 2 * (there - pixel_cols) + 1)
+        parity = (here == chosen).astype(jnp.float32).astype(jnp.bfloat16)
+        split = jnp.dot(
+            prior[0].reshape(heights * rows, cols), parity, preferred_element_type=jnp.float32
+        )
+        for kind in range(2):
+            sorted_cells[kind] = split[:, kind * pixel_cols : (kind + 1) * pixel_cols]
+        for kind in range(2):
+            for row in range(rows):
+                lines[kind, row + 4, :heights] = sorted_cells[
+                    kind, pl.ds(row, heights, stride=rows), :
+                ].astype(jnp.bfloat16)
+        east_ref[0] = jnp.zeros_like(east_ref[0])
+        west_ref[0] = jnp.zeros_like(west_ref[0])
+        lane = lax.broadcasted_iota(jnp.int32, (channels, pixel_cols), 1)
+        last = pixel_cols - 1
+        for row in range(-1, pixel_rows + 1):
+            even, odd = (
+                jnp.dot(
+                    taps[...],
+                    lines[kind, 2 * row + 2 : 2 * row + 7].reshape(5 * padded, pixel_cols),
+                    preferred_element_type=jnp.float32,
+                )
+                for kind, taps in ((0, even_ref), (1, odd_ref))
+            )
+            ahead = pltpu.roll(even[:channels] + odd[:channels], 1, 1)
+            behind = pltpu.roll(even[2 * channels :], last, 1)
+            inside = (
+                even[channels : 2 * channels]
+                + odd[channels:]
+                + jnp.where(lane == 0, 0.0, ahead)
+                + jnp.where(lane == last, 0.0, behind)
+            )
+            out[0, row + 1] = inside
+            at = 2 * (row + 2)
+            east = jnp.where(
+                (lane == at) | (lane == at + 1), pltpu.roll(inside, at + 2, 1), east_ref[0]
+            )
+            east_ref[0] = jnp.where(lane == 64 + at, pltpu.roll(ahead, 64 + at, 1), east)
+            west = jnp.where(
+                (lane == 64 + at) | (lane == 65 + at), pltpu.roll(inside, 64 + at, 1), west_ref[0]
+            )
+            west_ref[0] = jnp.where(
+                lane == at + 1, pltpu.roll(behind, (at + 2) % pixel_cols, 1), west
+            )
+
+    edge = jax.ShapeDtypeStruct((members, channels, pixel_cols), jnp.float32)
+    edge_spec = pl.BlockSpec((1, channels, pixel_cols), lambda i: (i, 0, 0))
+    return pl.pallas_call(
+        kernel,
+        grid=(members,),
+        out_shape=(
+            jax.ShapeDtypeStruct((members, pixel_rows + 2, channels, pixel_cols), jnp.float32),
+            edge,
+            edge,
+        ),
+        in_specs=[
+            pl.BlockSpec((1, heights, rows, cols), lambda i: (i, 0, 0, 0)),
+            pl.BlockSpec(even_taps.shape, lambda i: (0, 0)),
+            pl.BlockSpec(odd_taps.shape, lambda i: (0, 0)),
+        ],
+        out_specs=(
+            pl.BlockSpec((1, pixel_rows + 2, channels, pixel_cols), lambda i: (i, 0, 0, 0)),
+            edge_spec,
+            edge_spec,
+        ),
+        scratch_shapes=[
+            pltpu.VMEM((2, heights * rows, pixel_cols), jnp.float32),
+            pltpu.VMEM((2, rows + 8, padded, pixel_cols), jnp.bfloat16),
+        ],
+        compiler_params=pltpu.CompilerParams(vmem_limit_bytes=40 << 20),
+        name="entry_layer",
+    )(prior_states, even_taps, odd_taps)
+
+
+def end_fix(from_west, from_east, lane):
+    return jnp.where(lane % 2 == 0, from_west, pltpu.roll(from_east, 62, 1))
+
+
+def with_ends(values, fix, row, lane):
+    moved = pltpu.roll(fix, (60 - 2 * row) % 128, 1)
+    return values + jnp.where((lane == 0) | (lane == 127), moved, 0.0)
+
+
+def side_columns(from_west, from_east, own_east, own_west, lane):
+    return jnp.where(lane < 64, from_west + own_west, from_east + own_east)
+
+
+def row_ends(partial, own_east, own_west, from_west, from_east):
+    members, row_count, channels, pixel_cols = partial.shape
+    tail = row_count // SLOTS - 1
+
+    def kernel(top, bottom, east, west, left, right, north, south):
+        lane = lax.broadcasted_iota(jnp.int32, (channels, pixel_cols), 1)
+        for member in range(members):
+            inward, outward = left[member], right[member]
+            fix = end_fix(inward, outward, lane)
+            sides = side_columns(inward, outward, east[member], west[member], lane)
+            for slot in range(SLOTS):
+                north[member, slot] = with_ends(top[member, slot], fix, slot - 1, lane).astype(
+                    jnp.bfloat16
+                )
+                south[member, slot] = with_ends(
+                    bottom[member, slot], fix, row_count - 4 + slot, lane
+                ).astype(jnp.bfloat16)
+            north[member, SLOTS] = sides.astype(jnp.bfloat16)
+            south[member, SLOTS] = sides.astype(jnp.bfloat16)
+
+    edge_spec = pl.BlockSpec((members, channels, pixel_cols), lambda i: (0, 0, 0))
+    rows_spec = (members, SLOTS, channels, pixel_cols)
+    sent = (members, SLOTS + 1, channels, pixel_cols)
+    return pl.pallas_call(
+        kernel,
+        grid=(1,),
+        out_shape=(jax.ShapeDtypeStruct(sent, jnp.bfloat16),) * 2,
+        in_specs=[
+            pl.BlockSpec(rows_spec, lambda i: (0, 0, 0, 0)),
+            pl.BlockSpec(rows_spec, lambda i: (0, tail, 0, 0)),
+            edge_spec,
+            edge_spec,
+            edge_spec,
+            edge_spec,
+        ],
+        out_specs=(pl.BlockSpec(sent, lambda i: (0, 0, 0, 0)),) * 2,
+        compiler_params=pltpu.CompilerParams(vmem_limit_bytes=40 << 20),
+        name="row_ends",
+    )(partial, partial, own_east, own_west, from_west, from_east)
+
+
+def misfits(
+    borders, partial, own_east, own_west, from_west, from_east, from_north, from_south,
+    entry_offset, middle_taps, side_taps, middle_offset, matrix, offset, observed, variance, mask,
+):
+    members, row_count, channels, pixel_cols = partial.shape
+    pixel_rows = row_count - 2
+    bands = matrix.shape[0]
+
+    def kernel(
+        border, pre, east, west, left, right, above, below, bias_ref, taps, side, bias_two,
+        matrix_ref, offset_ref, obs, variance_ref, mask_ref, out, hidden, sides,
+    ):
+        lane = lax.broadcasted_iota(jnp.int32, (channels, pixel_cols), 1)
+        bias = bias_ref[...]
+        top, bottom = border[0] == 0, border[1] == 0
+        start, end = border[2] == 0, border[3] == 0
+        keep_top = jnp.where(top, 0.0, 1.0)
+        keep_bottom = jnp.where(bottom, 0.0, 1.0)
+        fix = end_fix(left[0], right[0], lane)
+
+        def level(values):
+            return jnp.maximum(values + bias, 0.0)
+
+        for row in range(-2, pixel_rows + 2):
+            if row == -2:
+                values = above[0, 0].astype(jnp.float32)
+            elif row == pixel_rows + 1:
+                values = below[0, SLOTS - 1].astype(jnp.float32)
+            else:
+                values = with_ends(pre[0, row + 1], fix, row, lane)
+                if row <= 0:
+                    values = values + above[0, row + 2].astype(jnp.float32)
+                if row >= pixel_rows - 1:
+                    values = values + below[0, row - pixel_rows + 1].astype(jnp.float32)
+            values = level(values)
+            if row < 0:
+                values = values * keep_top
+            if row >= pixel_rows:
+                values = values * keep_bottom
+            hidden[row + 2] = values.astype(jnp.bfloat16)
+
+        slot = lax.rem(lane, 64) // 2
+        cells = side_columns(left[0], right[0], east[0], west[0], lane)
+        upper = pltpu.roll(above[0, SLOTS].astype(jnp.float32), 128 - 2 * pixel_rows, 1)
+        lower = pltpu.roll(below[0, SLOTS].astype(jnp.float32), 2 * pixel_rows, 1)
+        cells = (
+            cells
+            + jnp.where(slot < 3, upper, 0.0)
+            + jnp.where((slot > pixel_rows) & (slot < pixel_rows + 4), lower, 0.0)
+        )
+        outside = (
+            (top & (slot < 2))
+            | (bottom & (slot >= pixel_rows + 2))
+            | (start & (lane < 64))
+            | (end & (lane >= 64))
+        )
+        cells = jnp.where(outside, 0.0, level(cells))
+        stack = jnp.concatenate(
+            [pltpu.roll(cells, 4, 1), cells, pltpu.roll(cells, 124, 1)], axis=0
+        ).astype(jnp.bfloat16)
+        found = jnp.dot(side[...], stack, preferred_element_type=jnp.float32)
+        sides[...] = jnp.where(lane < 64, found[:channels], found[channels:])
+
+        for row in range(pixel_rows):
+            window = jnp.concatenate([hidden[row], hidden[row + 2], hidden[row + 4]], axis=0)
+            parts = jnp.dot(taps[...], window, preferred_element_type=jnp.float32)
+            column = sides[...]
+            at = 2 * (row + 2)
+            values = (
+                parts[channels : 2 * channels]
+                + jnp.where(
+                    lane < 2,
+                    pltpu.roll(column, 128 - at, 1),
+                    pltpu.roll(parts[:channels], 2, 1),
+                )
+                + jnp.where(
+                    lane >= 126,
+                    pltpu.roll(column, 62 - at if at <= 62 else 190 - at, 1),
+                    pltpu.roll(parts[2 * channels :], 126, 1),
+                )
+            )
+            second = jnp.maximum(values + bias_two[...], 0.0).astype(jnp.bfloat16)
+            predicted = jnp.dot(matrix_ref[...], second, preferred_element_type=jnp.float32)
+            misfit = obs[row] - (predicted + offset_ref[...])
+            total = jnp.sum(misfit * misfit / variance_ref[...], axis=0, keepdims=True)
+            out[0, row : row + 1] = total * mask_ref[row : row + 1].astype(jnp.float32)
+
+    edge_spec = pl.BlockSpec((1, channels, pixel_cols), lambda i: (i, 0, 0))
+    line_spec = pl.BlockSpec((1, SLOTS + 1, channels, pixel_cols), lambda i: (i, 0, 0, 0))
+
+    def whole(array):
+        return pl.BlockSpec(array.shape, lambda i, n=array.ndim: (0,) * n)
+
+    fixed = (entry_offset, middle_taps, side_taps, middle_offset, matrix, offset, observed)
+    fixed = fixed + (variance, mask)
+    return pl.pallas_call(
+        kernel,
+        grid=(members,),
+        out_shape=jax.ShapeDtypeStruct((members, pixel_rows, pixel_cols), jnp.float32),
+        in_specs=[
+            pl.BlockSpec(memory_space=pltpu.SMEM),
+            pl.BlockSpec((1, row_count, channels, pixel_cols), lambda i: (i, 0, 0, 0)),
+            edge_spec,
+            edge_spec,
+            edge_spec,
+            edge_spec,
+            line_spec,
+            line_spec,
+        ]
+        + [whole(array) for array in fixed],
+        out_specs=pl.BlockSpec((1, pixel_rows, pixel_cols), lambda i: (i, 0, 0)),
+        scratch_shapes=[
+            pltpu.VMEM((pixel_rows + 4, channels, pixel_cols), jnp.bfloat16),
+            pltpu.VMEM((channels, pixel_cols), jnp.float32),
+        ],
+        compiler_params=pltpu.CompilerParams(vmem_limit_bytes=40 << 20),
+        name="misfits",
+    )(
+        borders, partial, own_east, own_west, from_west, from_east, from_north, from_south, *fixed
+    )
+
+
+def neighbours(axis):
+    count = lax.axis_size(axis)
+    onward = [(i, i + 1) for i in range(count - 1)]
+    return onward, [(j, i) for i, j in onward]
+
+
+def departures(
     prior_states,
     measured_brightness,
     measured_indicator,
@@ -312,44 +586,51 @@
     brightness_matrix,
     brightness_offset,
 ):
-    numbers = ("NCHW", "OIHW", "NCHW")
+    channels, heights = entry_layer_stencil.shape[:2]
+    padded = (heights + 15) // 16 * 16
+    entry = jnp.pad(entry_layer_stencil, ((0, 0), (0, padded - heights), (0, 0), (0, 0)))
+    entry = jnp.transpose(entry, (3, 0, 2, 1)).reshape(5, channels, 5 * padded)
+    even_taps = jnp.concatenate([entry[0], entry[2], entry[4]])
+    odd_taps = jnp.concatenate([entry[1], entry[3]])
+    middle = jnp.transpose(middle_layer_stencil, (3, 0, 2, 1)).reshape(3, channels, 3 * channels)
+    middle_taps = middle.reshape(3 * channels, 3 * channels)
+    side_taps = jnp.concatenate([middle[0], middle[2]])
+    lat, lon = lax.axis_index("lat"), lax.axis_index("lon")
+    borders = jnp.stack(
+        [lat, lax.axis_size("lat") - 1 - lat, lon, lax.axis_size("lon") - 1 - lon]
+    ).astype(jnp.int32)
+    partial, own_east, own_west = entry_layer(prior_states, even_taps, odd_taps)
+    onward, back = neighbours("lon")
+    from_west = lax.ppermute(own_east, "lon", onward)
+    from_east = lax.ppermute(own_west, "lon", back)
+    north, south = row_ends(partial, own_east, own_west, from_west, from_east)
+    onward, back = neighbours("lat")
+    from_north = lax.ppermute(south, "lat", onward)
+    from_south = lax.ppermute(north, "lat", back)
+    return misfits(
+        borders,
+        partial,
+        own_east,
+        own_west,
+        from_west,
+        from_east,
+        from_north,
+        from_south,
+        entry_layer_offset[:, None],
+        middle_taps,
+        side_taps,
+        middle_layer_offset[:, None],
+        brightness_matrix,
+        brightness_offset[:, None],
+        jnp.transpose(measured_brightness, (1, 0, 2)),
+        sensor_error_spread[:, None],
+        measured_indicator,
+    )
+
+
+def log_weights(*arguments):
     highest = lax.Precision.HIGHEST
-    enlarged_state = extended(prior_states, (("lat", 2), ("lon", 3)), 2)
-    first_layer = lax.conv_general_dilated(
-        enlarged_state,
-        entry_layer_stencil,
-        (2, 2),
-        "VALID",
-        dimension_numbers=numbers,
-        preferred_element_type=jnp.float32,
-    )
-    first_layer = jax.nn.relu(first_layer + entry_layer_offset[None, :, None, None]).astype(
-        jnp.bfloat16
-    )
-    first_wide = extended(first_layer, (("lat", 2), ("lon", 3)), 2)
-    second_layer = lax.conv_general_dilated(
-        first_wide,
-        middle_layer_stencil,
-        (1, 1),
-        "VALID",
-        rhs_dilation=(2, 2),
-        dimension_numbers=numbers,
-        preferred_element_type=jnp.float32,
-    )
-    second_layer = jax.nn.relu(second_layer + middle_layer_offset[None, :, None, None]).astype(
-        jnp.bfloat16
-    )
-    predicted = (
-        jnp.einsum(
-            "oc,pcij->poij", brightness_matrix, second_layer, preferred_element_type=jnp.float32
-        )
-        + brightness_offset[None, :, None, None]
-    )
-    innovation = measured_brightness[None] - predicted
-    departure_power_two = (
-        jnp.sum(innovation * innovation / sensor_error_spread[None, :, None, None], axis=1)
-        * measured_indicator.astype(jnp.float32)[None]
-    )
+    departure_power_two = departures(*arguments)
     band_lat = taper_band(departure_power_two.shape[1], RADIUS)
     band_lon = taper_band(departure_power_two.shape[2], RADIUS)
     padded = extended(departure_power_two, (("lat", 1),), RADIUS)

time: 263 us -> 134 us (0.51)
  matrix products: 52.7 us -> 1.84 us
  Pallas kernels: 93.8 us -> 62.6 us
  waiting for transfers between devices: 57.6 us -> 28.7 us
  local copies, waits for them, and re-layouts: 21.4 us -> 12.4 us
  starting transfers between devices: 32.5 us -> 24.7 us
    pallas_call x1, Pallas kernels: 81.4 us -> 2.82 us  [pick_tiles(): pl.pallas_call(kernel, out_shape=jax.ShapeDtypeStruct((targets, seats, he...]
    conv_general_dilated x2 -> x0, matrix products: 49.6 us -> none  [the longest x1 36.2 us: log_weights(): lax.conv_general_dilated(enlarged_state, entry_layer_stencil, (2, 2), 'VA...]
    pallas_call x0 -> x3, Pallas kernels: none -> 47.5 us  [the longest x1 23.5 us: misfits(): pl.pallas_call(kernel, grid=(members,), out_shape=jax.ShapeDtypeStruct((m...]
    ppermute x1, waiting for transfers between devices: 33.2 us -> 14.1 us  [body(): other_norm = lax.ppermute(own_norm, 'ens', swap)]
    ppermute x6 -> x2, waiting for transfers between devices: 15.9 us -> 1.84 us  [extended(): after = lax.ppermute(first, axis, down)]
    ppermute x0 -> x4, waiting for transfers between devices: none -> 11.5 us  [the longest x1 4.6 us: departures(): from_south = lax.ppermute(north, 'lat', back)]
    ppermute x6 -> x2, starting transfers between devices: 20.9 us -> 9.52 us  [extended(): before = lax.ppermute(last, axis, up)]
    ppermute x0 -> x4, starting transfers between devices: none -> 7.55 us  [the longest x1 3.5 us: departures(): from_north = lax.ppermute(south, 'lat', onward)]
  transfers between devices with their start and end apart: 15 -> 11, of which waited for: 7 -> 6; matrix products, arithmetic and copies ran while one was open for 13% -> 5% of each run, Pallas kernels for 32% -> 39%
where the time goes in v1:
time: 134 us; the launch traced here: 132 us
  Pallas kernels  62.6 us (47%)
  waiting for transfers between devices  28.7 us (21%)
  starting transfers between devices  24.7 us (18%)
  local copies, waits for them, and re-layouts  12.4 us (9%)
  matrix products  1.84 us (1%)
    pallas_call x1, Pallas kernels, misfits(): pl.pallas_call(kernel, grid=(members,), out_shape=jax.ShapeDtypeStruct((m...  23.5 us
    pallas_call x1, Pallas kernels, entry_layer(): pl.pallas_call(kernel, grid=(members,), out_shape=(jax.ShapeDtypeStruct((...  22.1 us
    ppermute x1, waiting for transfers between devices, body(): other_norm = lax.ppermute(own_norm, 'ens', swap)  14.1 us
    ppermute x2, starting transfers between devices, extended(): before = lax.ppermute(last, axis, up)  9.52 us
    unnamed x30, local copies, waits for them, and re-layouts  9.1 us
    pallas_call x1, Pallas kernels, combine(): pl.pallas_call(kernel, grid=(steps,), out_shape=(jax.ShapeDtypeStruct(pri...  8.64 us
    ppermute x1, waiting for transfers between devices, departures(): from_south = lax.ppermute(north, 'lat', back)  4.6 us
    ppermute x1, waiting for transfers between devices, departures(): from_east = lax.ppermute(own_west, 'lon', back)  3.69 us
  transfers between devices with their start and end apart: 11, of which 6 were waited for; matrix products, arithmetic and copies ran while one was open for 5% of the time, Pallas kernels for 39%

profile of v1, /device:TPU:0, one launch (start us, length us, event | category | flops | bytes accessed | tf_op | source)
XLA Modules:
  0.0 132.2 jit_solution(12405400857181588825)
XLA Ops:
  0.6 0.8 copy.27
  1.4 0.1 reshape.26.ancestor
  1.6 2.5 %copy-done = bf16[8,40,32,256]{3,2,1,0:T(8,128)(2,1)S(1)} copy-done((bf16[8,40,32,256]{3,2,1,0:T(8,128)(2,1)S(1)}, bf16[8,40,32,256]{3,2,1,0:T(8,128)(2,1)}, u32[]{:S(2)}) %copy-start) | copy-done | bytes 5242904
  4.0 2.8 %pick_tiles.1 = bf16[1,4,40,32,256]{4,3,2,1,0:T(8,128)(2,1)} custom-call(s32[32]{0:T(128)S(1)} %reshape.26.ancestor, s32[2]{0:T(128)S(1)} %pad_add_fusion.spot, bf16[8,40,32,256]{3,2,1,0:T(8,128)(2,1)S(1)} %copy-done), custom_call_target="tpu_custom_call" | custom-call | tf_op jit(solution)/shard_map/pick_tiles/pallas_call | solution.py:116
  6.9 3.0 %collective-permute-start.10 = (bf16[1,4,40,32,256]{4,3,2,1,0:T(8,128)(2,1)}, bf16[1,4,40,32,256]{4,3,2,1,0:T(8,128)(2,1)}, u32[]{:S(2)}, u32[]{:S(2)}) collective-permute-start(bf16[1,4,40,32,256]{4,3,2,1,0:T(8,128)(2,1)} %pick_tiles.1), channel_id=1, source_target_pairs={{0,16},{16,0},{1,17},{17,1},{2,18},{18,2},{3,19},{19,3},{4,20},{20... | collective-permute-start | bytes 7864328 | tf_op jit(solution)/shard_map/ppermute | solution.py:663
  10.0 0.1 copy.31
  10.1 0.1 copy.32
  10.2 0.1 copy.30
  10.3 0.1 copy.29
  10.4 0.1 copy.28
  10.5 2.5 %copy-done.1 = bf16[8,40,32,256]{3,2,1,0:T(8,128)(2,1)S(1)} copy-done((bf16[8,40,32,256]{3,2,1,0:T(8,128)(2,1)S(1)}, bf16[8,40,32,256]{3,2,1,0:T(8,128)(2,1)}, u32[]{:S(2)}) %copy-start.1) | copy-done | bytes 5242904
  13.0 22.1 %entry_layer.1 = (f32[8,18,64,128]{3,2,1,0:T(8,128)S(1)}, f32[8,64,128]{2,1,0:T(8,128)S(1)}, f32[8,64,128]{2,1,0:T(8,128)S(1)}) custom-call(bf16[8,40,32,256]{3,2,1,0:T(8,128)(2,1)S(1)} %copy-done.1, bf16[192,240]{1,0:T(8,128)(2,1)S(1)} %pad_maximum_fusion.even_ref, bf16[128,240]{1,0:T(8,128)(2,1)S(1)} %pad_maximum_fusion.1.odd_ref), custom_call_target="tpu_custom_call" | custom-call | tf_op jit(solution)/shard_map/entry_layer/pallas_call | solution.py:368
  35.1 1.5 %collective-permute-start = (f32[8,64,128]{2,1,0:T(8,128)S(1)}, f32[8,64,128]{2,1,0:T(8,128)S(1)}, u32[]{:S(2)}, u32[]{:S(2)}) collective-permute-start(f32[8,64,128]{2,1,0:T(8,128)S(1)} %get-tuple-element.12.east), channel_id=1, source_target_pairs={{0,1},{1,2},{2,3},{4,5},{5,6},{6,7},{8,9},{9,10},{10,11},{12,13},{... | collective-permute-start | bytes 786440 | tf_op jit(solution)/shard_map/ppermute | solution.py:604
  36.6 1.3 collective-permute-start.1
  37.9 3.7 %collective-permute-done.1.right = f32[8,64,128]{2,1,0:T(8,128)S(1)} collective-permute-done((f32[8,64,128]{2,1,0:T(8,128)S(1)}, f32[8,64,128]{2,1,0:T(8,128)S(1)}, u32[]{:S(2)}, u32[]{:S(2)}) %collective-permute-start.1) | collective-permute-done | bytes 262176 | tf_op jit(solution)/shard_map/ppermute | solution.py:605
  41.7 1.9 %row_ends.1 = (bf16[8,4,64,128]{3,2,1,0:T(8,128)(2,1)}, bf16[8,4,64,128]{3,2,1,0:T(8,128)(2,1)}) custom-call(f32[8,18,64,128]{3,2,1,0:T(8,128)S(1)} %get-tuple-element.11.top.bottom.pre, f32[8,18,64,128]{3,2,1,0:T(8,128)S(1)} %get-tuple-element.11.top.bottom.pre, f32[8,64,128]{2,1,0:T(8,128)S(1)} %get-tuple-element.12.east, ...), custom_call_target="tpu_custom_call" | custom-call | tf_op jit(solution)/shard_map/row_ends/pallas_call | solution.py:431
  43.6 3.5 %collective-permute-start.2 = (bf16[8,4,64,128]{3,2,1,0:T(8,128)(2,1)}, bf16[8,4,64,128]{3,2,1,0:T(8,128)(2,1)S(1)}, u32[]{:S(2)}, u32[]{:S(2)}) collective-permute-start(bf16[8,4,64,128]{3,2,1,0:T(8,128)(2,1)} %get-tuple-element.14), channel_id=1, source_target_pairs={{0,4},{4,8},{8,12},{1,5},{5,9},{9,13},{2,6},{6,10},{10,14},{3,7},{... | collective-permute-start | bytes 1572872 | tf_op jit(solution)/shard_map/ppermute | solution.py:608
  47.1 1.3 collective-permute-start.3
  48.4 0.1 copy.42.variance_ref
  48.5 0.1 copy.41.offset_ref
  48.6 0.1 copy.39.bias_ref
  48.7 0.1 copy.40.bias_two
  48.8 0.8 copy.33
  49.6 0.1 copy.34
  49.7 0.1 copy.36
  49.8 0.1 copy.35
  49.9 0.1 copy.37
  50.0 1.0 copy.44
  51.0 1.1 reshape_reshape.3.taps
  52.2 3.2 %collective-permute-done.2.above = bf16[8,4,64,128]{3,2,1,0:T(8,128)(2,1)S(1)} collective-permute-done((bf16[8,4,64,128]{3,2,1,0:T(8,128)(2,1)}, bf16[8,4,64,128]{3,2,1,0:T(8,128)(2,1)S(1)}, u32[]{:S(2)}, u32[]{:S(2)}) %collective-permute-start.2) | collective-permute-done | bytes 524320 | tf_op jit(solution)/shard_map/ppermute | solution.py:608
  55.4 4.6 %collective-permute-done.3.below = bf16[8,4,64,128]{3,2,1,0:T(8,128)(2,1)S(1)} collective-permute-done((bf16[8,4,64,128]{3,2,1,0:T(8,128)(2,1)}, bf16[8,4,64,128]{3,2,1,0:T(8,128)(2,1)S(1)}, u32[]{:S(2)}, u32[]{:S(2)}) %collective-permute-start.3) | collective-permute-done | bytes 524320 | tf_op jit(solution)/shard_map/ppermute | solution.py:609
  60.0 2.3 %copy-done.3 = f32[8,18,64,128]{3,2,1,0:T(8,128)S(1)} copy-done((f32[8,18,64,128]{3,2,1,0:T(8,128)S(1)}, f32[8,18,64,128]{3,2,1,0:T(8,128)}, u32[]{:S(2)}) %copy-start.3) | copy-done | bytes 4718616
  62.4 23.5 %misfits.1 = f32[8,16,128]{2,1,0:T(8,128)S(1)} custom-call(s32[4]{0:T(128)S(1)} %pad_add_fusion.1.border, f32[8,18,64,128]{3,2,1,0:T(8,128)S(1)} %copy-done.3, f32[8,64,128]{2,1,0:T(8,128)S(1)} %get-tuple-element.12.east, f32[8,64,128]{2,1,0:T(8,128)S(1)} %get-tuple-element.13.west, f32[8,64,128]{2,1,0:T(8,128)S(1)} %collective-permute-done.left, ...), custom_call_target="tpu_custom_call" | custom-call | tf_op jit(solution)/shard_map/misfits/pallas_call | solution.py:544
  85.8 1.3 collective-permute-start.5
  87.1 4.5 %collective-permute-start.4 = (f32[8,16,128]{2,1,0:T(8,128)S(1)}, f32[8,16,128]{2,1,0:T(8,128)S(1)}, u32[]{:S(2)}, u32[]{:S(2)}) collective-permute-start(f32[8,16,128]{2,1,0:T(8,128)S(1)} %misfits.1), channel_id=1, source_target_pairs={{0,4},{4,8},{8,12},{1,5},{5,9},{9,13},{2,6},{6,10},{10,14},{3,7},{... | collective-permute-start | bytes 196616 | tf_op jit(solution)/shard_map/ppermute | solution.py:25
  91.7 0.6 exponential_reduce_fusion
  92.3 1.3 collective-permute-done.4
  93.6 0.9 convolution_bitcast_fusion
  94.5 0.1 fusion.68
  94.5 5.0 %collective-permute-start.6 = (f32[8,16,16]{2,1,0:T(8,128)S(1)}, f32[8,16,16]{2,1,0:T(8,128)S(1)}, u32[]{:S(2)}, u32[]{:S(2)}) collective-permute-start(f32[8,16,16]{2,1,0:T(8,128)S(1)} %get-tuple-element.27), channel_id=1, source_target_pairs={{0,1},{1,2},{2,3},{4,5},{5,6},{6,7},{8,9},{9,10},{10,11},{12,13},{... | collective-permute-start | bytes 24584 | tf_op jit(solution)/shard_map/ppermute | solution.py:25
  99.5 1.3 collective-permute-start.7
  100.8 1.8 %collective-permute-done.7 = f32[8,16,16]{2,1,0:T(8,128)S(1)} collective-permute-done((f32[8,16,16]{2,1,0:T(8,128)S(1)}, f32[8,16,16]{2,1,0:T(8,128)S(1)}, u32[]{:S(2)}, u32[]{:S(2)}) %collective-permute-start.7) | collective-permute-done | bytes 8224 | tf_op jit(solution)/shard_map/ppermute | solution.py:26
  102.7 1.0 convolution_multiply_fusion.log_ref
  103.7 3.7 %group_mean.1 = (f32[8,16,128]{2,1,0:T(8,128)S(1)}, f32[2,16,128]{2,1,0:T(8,128)S(1)}, f32[40,32,256]{2,1,0:T(8,128)S(1)}, bf16[40,32,256]{2,1,0:T(8,128)(2,1)S(1)}) custom-call(f32[8,16,128]{2,1,0:T(8,128)S(1)} %convolution_multiply_fusion.log_ref, bf16[8,40,32,256]{3,2,1,0:T(8,128)(2,1)S(1)} %bitcast.35), custom_call_target="tpu_custom_call" | custom-call | tf_op jit(solution)/shard_map/group_mean/pallas_call | solution.py:155
  107.3 0.6 collective-permute-start.9
  107.9 1.5 %collective-permute-start.8 = (f32[2,16,128]{2,1,0:T(8,128)S(1)}, f32[2,16,128]{2,1,0:T(8,128)S(1)}, u32[]{:S(2)}, u32[]{:S(2)}) collective-permute-start(f32[2,16,128]{2,1,0:T(8,128)S(1)} %get-tuple-element.17.own_ref), channel_id=1, source_target_pairs={{0,16},{16,0},{1,17},{17,1},{2,18},{18,2},{3,19},{19,3},{4,20},{20... | collective-permute-start | bytes 49160 | tf_op jit(solution)/shard_map/ppermute | solution.py:671
  109.4 14.1 %collective-permute-done.8.other_ref = f32[2,16,128]{2,1,0:T(8,128)S(1)} collective-permute-done((f32[2,16,128]{2,1,0:T(8,128)S(1)}, f32[2,16,128]{2,1,0:T(8,128)S(1)}, u32[]{:S(2)}, u32[]{:S(2)}) %collective-permute-start.8) | collective-permute-done | bytes 16416 | tf_op jit(solution)/shard_map/ppermute | solution.py:671
  123.5 8.6 %combine.1 = (f32[8,40,32,256]{3,2,1,0:T(8,128)}, f32[8,16,128]{2,1,0:T(8,128)}) custom-call(s32[32]{0:T(128)S(1)} %reshape.26.ancestor, s32[2]{0:T(128)S(1)} %pad_add_fusion.spot, f32[8,16,128]{2,1,0:T(8,128)S(1)} %get-tuple-element.16.scaled_ref, f32[2,16,128]{2,1,0:T(8,128)S(1)} %get-tuple-element.17.own_ref, ...), custom_call_target="tpu_custom_call" | custom-call | tf_op jit(solution)/shard_map/combine/pallas_call | solution.py:267
  (39 shorter events, 0.4 us)
Async XLA Ops:
  1.6 2.5 %copy-start = (bf16[8,40,32,256]{3,2,1,0:T(8,128)(2,1)S(1)}, bf16[8,40,32,256]{3,2,1,0:T(8,128)(2,1)}, u32[]{:S(2)}) copy-start(bf16[8,40,32,256]{3,2,1,0:T(8,128)(2,1)} %prior.7) | copy-start | bytes 15728644
  4.0 5.8 %copy-start.7 = (bf16[64,40,5,5]{0,1,3,2:T(8,128)(2,1)S(1)}, bf16[64,40,5,5]{0,1,3,2:T(8,128)(2,1)}, u32[]{:S(2)}) copy-start(bf16[64,40,5,5]{0,1,3,2:T(8,128)(2,1)} %param.15) | copy-start | bytes 384004
  6.9 116.7 %collective-permute-start.10 = (bf16[1,4,40,32,256]{4,3,2,1,0:T(8,128)(2,1)}, bf16[1,4,40,32,256]{4,3,2,1,0:T(8,128)(2,1)}, u32[]{:S(2)}, u32[]{:S(2)}) collective-permute-start(bf16[1,4,40,32,256]{4,3,2,1,0:T(8,128)(2,1)} %pick_tiles.1), channel_id=1, source_target_pairs={{0,16},{16,0},{1,17},{17,1},{2,18},{18,2},{3,19},{19,3},{4,20},{20... | collective-permute-start | bytes 7864328 | tf_op jit(solution)/shard_map/ppermute | solution.py:663
  10.5 2.5 %copy-start.1 = (bf16[8,40,32,256]{3,2,1,0:T(8,128)(2,1)S(1)}, bf16[8,40,32,256]{3,2,1,0:T(8,128)(2,1)}, u32[]{:S(2)}) copy-start(bf16[8,40,32,256]{3,2,1,0:T(8,128)(2,1)} %prior.7) | copy-start | bytes 15728644
  35.1 8.5 %copy-start.2 = (f32[8,18,64,128]{3,2,1,0:T(8,128)}, f32[8,18,64,128]{3,2,1,0:T(8,128)S(1)}, u32[]{:S(2)}) copy-start(f32[8,18,64,128]{3,2,1,0:T(8,128)S(1)} %get-tuple-element.11.top.bottom.pre) | copy-start | bytes 14155780
  35.1 2.8 %collective-permute-start = (f32[8,64,128]{2,1,0:T(8,128)S(1)}, f32[8,64,128]{2,1,0:T(8,128)S(1)}, u32[]{:S(2)}, u32[]{:S(2)}) collective-permute-start(f32[8,64,128]{2,1,0:T(8,128)S(1)} %get-tuple-element.12.east), channel_id=1, source_target_pairs={{0,1},{1,2},{2,3},{4,5},{5,6},{6,7},{8,9},{9,10},{10,11},{12,13},{... | collective-permute-start | bytes 786440 | tf_op jit(solution)/shard_map/ppermute | solution.py:604
  36.6 5.0 %collective-permute-start.1 = (f32[8,64,128]{2,1,0:T(8,128)S(1)}, f32[8,64,128]{2,1,0:T(8,128)S(1)}, u32[]{:S(2)}, u32[]{:S(2)}) collective-permute-start(f32[8,64,128]{2,1,0:T(8,128)S(1)} %get-tuple-element.13.west), channel_id=1, source_target_pairs={{1,0},{2,1},{3,2},{5,4},{6,5},{7,6},{9,8},{10,9},{11,10},{13,12},{... | collective-permute-start | bytes 786440 | tf_op jit(solution)/shard_map/ppermute | solution.py:605
  41.6 6.8 %copy-start.10 = (f32[16]{0:T(128)S(1)}, f32[16]{0:T(128)}, u32[]{:S(2)}) copy-start(f32[16]{0:T(128)} %param.14) | copy-start | bytes 196
  41.6 6.9 %copy-start.11 = (f32[16]{0:T(128)S(1)}, f32[16]{0:T(128)}, u32[]{:S(2)}) copy-start(f32[16]{0:T(128)} %param.20) | copy-start | bytes 196
  41.6 7.0 %copy-start.8 = (f32[64]{0:T(128)S(1)}, f32[64]{0:T(128)}, u32[]{:S(2)}) copy-start(f32[64]{0:T(128)} %param.16) | copy-start | bytes 772
  41.6 7.0 %copy-start.9 = (f32[64]{0:T(128)S(1)}, f32[64]{0:T(128)}, u32[]{:S(2)}) copy-start(f32[64]{0:T(128)} %param.18) | copy-start | bytes 772
  41.6 7.1 %copy-start.6 = (bf16[64,64,3,3]{1,0,3,2:T(8,128)(2,1)S(1)}, bf16[64,64,3,3]{1,0,3,2:T(8,128)(2,1)}, u32[]{:S(2)}) copy-start(bf16[64,64,3,3]{1,0,3,2:T(8,128)(2,1)} %param.17) | copy-start | bytes 221188
  41.6 18.4 %copy-start.4 = (s32[16,128]{1,0:T(8,128)S(1)}, s32[16,128]{1,0:T(8,128)}, u32[]{:S(2)}) copy-start(s32[16,128]{1,0:T(8,128)} %mask_ref.1) | copy-start | bytes 24580
  41.6 18.4 %copy-start.5 = (bf16[16,64]{1,0:T(8,128)(2,1)S(1)}, bf16[16,64]{1,0:T(8,128)(2,1)}, u32[]{:S(2)}) copy-start(bf16[16,64]{1,0:T(8,128)(2,1)} %matrix_ref.1) | copy-start | bytes 6148
  43.6 11.8 %collective-permute-start.2 = (bf16[8,4,64,128]{3,2,1,0:T(8,128)(2,1)}, bf16[8,4,64,128]{3,2,1,0:T(8,128)(2,1)S(1)}, u32[]{:S(2)}, u32[]{:S(2)}) collective-permute-start(bf16[8,4,64,128]{3,2,1,0:T(8,128)(2,1)} %get-tuple-element.14), channel_id=1, source_target_pairs={{0,4},{4,8},{8,12},{1,5},{5,9},{9,13},{2,6},{6,10},{10,14},{3,7},{... | collective-permute-start | bytes 1572872 | tf_op jit(solution)/shard_map/ppermute | solution.py:608
  47.1 12.9 %collective-permute-start.3 = (bf16[8,4,64,128]{3,2,1,0:T(8,128)(2,1)}, bf16[8,4,64,128]{3,2,1,0:T(8,128)(2,1)S(1)}, u32[]{:S(2)}, u32[]{:S(2)}) collective-permute-start(bf16[8,4,64,128]{3,2,1,0:T(8,128)(2,1)} %get-tuple-element.15), channel_id=1, source_target_pairs={{4,0},{8,4},{12,8},{5,1},{9,5},{13,9},{6,2},{10,6},{14,10},{7,3},{... | collective-permute-start | bytes 1572872 | tf_op jit(solution)/shard_map/ppermute | solution.py:609
  49.7 53.9 %slice-start = ((s8[5242880]{0:T(1024)(128)(4,1)}), s8[1048576]{0:T(1024)(128)(4,1)S(1)}, s32[]{:S(2)}) async-start(s8[5242880]{0:T(1024)(128)(4,1)} %bitcast.34), calls=%async_computation | async-start | bytes 2097152
  60.0 2.3 %copy-start.3 = (f32[8,18,64,128]{3,2,1,0:T(8,128)S(1)}, f32[8,18,64,128]{3,2,1,0:T(8,128)}, u32[]{:S(2)}) copy-start(f32[8,18,64,128]{3,2,1,0:T(8,128)} %copy-done.2) | copy-start | bytes 14155780
  62.3 41.3 %slice-start.1 = ((s8[5242880]{0:T(1024)(128)(4,1)}), s8[4194304]{0:T(1024)(128)(4,1)S(1)}, s32[]{:S(2)}) async-start(s8[5242880]{0:T(1024)(128)(4,1)} %bitcast.34), calls=%async_computation.1 | async-start | bytes 8388608
  85.8 6.5 %collective-permute-start.5 = (f32[8,16,128]{2,1,0:T(8,128)S(1)}, f32[8,16,128]{2,1,0:T(8,128)S(1)}, u32[]{:S(2)}, u32[]{:S(2)}) collective-permute-start(f32[8,16,128]{2,1,0:T(8,128)S(1)} %misfits.1), channel_id=1, source_target_pairs={{4,0},{8,4},{12,8},{5,1},{9,5},{13,9},{6,2},{10,6},{14,10},{7,3},{... | collective-permute-start | bytes 196616 | tf_op jit(solution)/shard_map/ppermute | solution.py:26
  87.1 6.4 %collective-permute-start.4 = (f32[8,16,128]{2,1,0:T(8,128)S(1)}, f32[8,16,128]{2,1,0:T(8,128)S(1)}, u32[]{:S(2)}, u32[]{:S(2)}) collective-permute-start(f32[8,16,128]{2,1,0:T(8,128)S(1)} %misfits.1), channel_id=1, source_target_pairs={{0,4},{4,8},{8,12},{1,5},{5,9},{9,13},{2,6},{6,10},{10,14},{3,7},{... | collective-permute-start | bytes 196616 | tf_op jit(solution)/shard_map/ppermute | solution.py:25
  94.5 6.3 %collective-permute-start.6 = (f32[8,16,16]{2,1,0:T(8,128)S(1)}, f32[8,16,16]{2,1,0:T(8,128)S(1)}, u32[]{:S(2)}, u32[]{:S(2)}) collective-permute-start(f32[8,16,16]{2,1,0:T(8,128)S(1)} %get-tuple-element.27), channel_id=1, source_target_pairs={{0,1},{1,2},{2,3},{4,5},{5,6},{6,7},{8,9},{9,10},{10,11},{12,13},{... | collective-permute-start | bytes 24584 | tf_op jit(solution)/shard_map/ppermute | solution.py:25
  99.5 3.1 %collective-permute-start.7 = (f32[8,16,16]{2,1,0:T(8,128)S(1)}, f32[8,16,16]{2,1,0:T(8,128)S(1)}, u32[]{:S(2)}, u32[]{:S(2)}) collective-permute-start(f32[8,16,16]{2,1,0:T(8,128)S(1)} %get-tuple-element.28), channel_id=1, source_target_pairs={{1,0},{2,1},{3,2},{5,4},{6,5},{7,6},{9,8},{10,9},{11,10},{13,12},{... | collective-permute-start | bytes 24584 | tf_op jit(solution)/shard_map/ppermute | solution.py:26
  107.3 16.2 %collective-permute-start.9 = (bf16[40,32,256]{2,1,0:T(8,128)(2,1)S(1)}, bf16[40,32,256]{2,1,0:T(8,128)(2,1)S(1)}, u32[]{:S(2)}, u32[]{:S(2)}) collective-permute-start(bf16[40,32,256]{2,1,0:T(8,128)(2,1)S(1)} %get-tuple-element.19), channel_id=1, source_target_pairs={{0,16},{16,0},{1,17},{17,1},{2,18},{18,2},{3,19},{19,3},{4,20},{20... | collective-permute-start | bytes 1966088 | tf_op jit(solution)/shard_map/ppermute | solution.py:672
  107.9 15.6 %collective-permute-start.8 = (f32[2,16,128]{2,1,0:T(8,128)S(1)}, f32[2,16,128]{2,1,0:T(8,128)S(1)}, u32[]{:S(2)}, u32[]{:S(2)}) collective-permute-start(f32[2,16,128]{2,1,0:T(8,128)S(1)} %get-tuple-element.17.own_ref), channel_id=1, source_target_pairs={{0,16},{16,0},{1,17},{17,1},{2,18},{18,2},{3,19},{19,3},{4,20},{20... | collective-permute-start | bytes 49160 | tf_op jit(solution)/shard_map/ppermute | solution.py:671
